TPU v7x, 256 devices: a whole 4x4x8 slice. The times are simulated.
256 devices in a mesh: chan: 32 (over z, x_lo, core), day: 8 (over x_hi, y).
Axes of the slice: x: 4 (x_hi: 2, x_lo: 2; x = x_hi * 2 + x_lo), y: 4, z: 8, core: 2. Of those that a mesh axis runs over, the one named last changes fastest.
Arguments:
- spectra: bfloat16 [8, 512, 2, 4096], P('day', 'chan'), may hold values from -6 to 6
- source_index: int32 [16], replicated, may hold values from 0 to 511, as said below
- interrogator: int32 [512], P('chan'), may hold values from 0 to 7, as said below
- lag_bounds: int32 [16, 2], replicated, may hold values from 0 to 256, as said below
Outputs:
- reference_stack: bfloat16 [16, 512, 256], P('day', 'chan')
- drift: float32 [8, 8], P('day')
Inputs may be any that keep to these rules, and one draw needn't show every extreme that they name: `source_index`: distinct channels. Each interrogator serves one contiguous run of channels, in rising order, of at least 32 channels. `lag_bounds`: first lag below end lag, and each window spans at least 128 lags.
All inputs are finite; a program needn't handle non-finite values.
Results may differ from a plain program's by a relative error of at most 0.0065.
Values may be sent and summed in bfloat16 or wider, within the bound.
No kernel may reach another device: no remote copies, remote signals or barrier semaphores. Data moves between devices by JAX's collectives and lax.ppermute only.
A program may use at most 64 MiB of HBM per device.

v0:
```python
import math
import jax
import jax.numpy as jnp
from jax import lax
from jax.sharding import PartitionSpec as P

LAGS = 256
NINT = 8


def from_root(value, axis, source):
    kept = jnp.where(lax.axis_index(axis) == source, value, 0).astype(value.dtype)
    return lax.psum(kept, axis)


def lag_table(bins, lags):
    freq = jnp.arange(bins, dtype=jnp.int32)
    shift = jnp.arange(lags, dtype=jnp.int32) - lags // 2
    phase = freq[:, None] * shift[None, :] % (2 * bins)
    angle = math.pi * phase.astype(jnp.float32) / bins
    scale = 1.0 / math.sqrt(bins)
    return jnp.concatenate([jnp.cos(angle) * scale, -jnp.sin(angle) * scale], 0).astype(
        jnp.bfloat16
    )


def per_device(spectra, source_index, interrogator, lag_bounds):
    day_dev, ch_dev, _, bins = spectra.shape
    nsrc = source_index.shape[0]
    lags = LAGS

    def fetch(source, buffer):
        chosen_chan = source_index[source]
        owner = chosen_chan // ch_dev
        local_row = chosen_chan - owner * ch_dev
        piece = lax.dynamic_slice_in_dim(spectra, local_row, 1, 1)
        arrived = from_root(piece, "chan", owner)
        return lax.dynamic_update_slice_in_dim(buffer, arrived, source, 1)

    sources = lax.fori_loop(0, nsrc, fetch, jnp.zeros((day_dev, nsrc, 2, bins), jnp.bfloat16))
    table = lag_table(bins, lags)
    block = math.gcd(nsrc, 16)

    def correlate_block(index, corr):
        chosen = sources[0].astype(jnp.float32)
        local = spectra[0].astype(jnp.float32)
        real_in = local[None, :, 0]
        imag_in = local[None, :, 1]
        real_src = chosen[:, None, 0]
        imag_src = chosen[:, None, 1]
        cross = jnp.concatenate(
            [real_in * real_src + imag_in * imag_src, imag_in * real_src - real_in * imag_src], -1
        )
        cross = cross.astype(jnp.bfloat16).reshape(block * ch_dev, 2 * bins)
        result = jnp.dot(cross, table, preferred_element_type=jnp.float32).reshape(
            1, block, ch_dev, lags
        )
        return result

    corr = lax.fori_loop(
        0, nsrc // block, correlate_block, jnp.zeros((day_dev, nsrc, ch_dev, lags), jnp.float32)
    )
    local_sum = jnp.sum(corr, 0)
    days = day_dev * lax.axis_size("day")
    total = lax.psum(local_sum, "day")
    ref_full = (total / days).astype(jnp.bfloat16)
    share = nsrc // lax.axis_size("day")
    ref_out = lax.dynamic_slice_in_dim(ref_full, lax.axis_index("day") * share, share, 0)
    ref_float = ref_full.astype(jnp.float32)
    lag_pos = jnp.arange(lags, dtype=jnp.int32)
    window = (
        (lag_pos[None, :] >= lag_bounds[:, 0:1]) & (lag_pos[None, :] < lag_bounds[:, 1:2])
    ).astype(jnp.float32)
    member = (interrogator[:, None] == jnp.arange(NINT, dtype=jnp.int32)[None, :]).astype(
        jnp.float32
    )
    day_corr = corr[0]
    padded = jnp.pad(day_corr, ((0, 0), (0, 0), (1, 1)))
    slope = 0.5 * (padded[:, :, 2:] - padded[:, :, :-2])
    weighted = window[:, None, :] * slope
    num_chan = jnp.sum(weighted * (day_corr - ref_float), axis=(0, 2))
    den_chan = jnp.sum(weighted * slope, axis=(0, 2))
    numers = [jnp.sum(num_chan[:, None] * member, 0)]
    denoms = [jnp.sum(den_chan[:, None] * member, 0)]
    numer, denom = lax.psum((jnp.stack(numers, 0), jnp.stack(denoms, 0)), "chan")
    drift = numer / (denom + 1e-06)
    return (ref_out, drift)


def solution(mesh):
    return jax.shard_map(
        per_device,
        mesh=mesh,
        in_specs=(P("day", "chan", None, None), P(), P("chan"), P()),
        out_specs=(P("day", "chan", None), P("day", None)),
        check_vma=False,
    )
```

profile of v0, /device:TPU:1, one launch (start us, length us, event | category | flops | bytes accessed | tf_op | source)
XLA Modules:
  0.0 1944.4 jit_solution(5148934047910936278)
XLA Ops:
  9.0 1759.0 %while.19 = (s32[]{:T(128)}, bf16[1,16,2,4096]{3,2,1,0:T(2,128)(2,1)S(1)}, s32[16]{0:T(128)}, bf16[1,16,2,4096]{3,2,1,0:T(2,128)(2,1)}, s32[]{:T(128)}, /*index=...) while((s32[]{:T(128)}, ...), condition=%wide.region_2.3_spmd, body=%wide.region_0.2_spmd.sunk | while | flops 16410 | bytes 98691 | solution.py:40
  9.0 1.2 dynamic_slice.29
  14.2 107.7 %psum.39 = bf16[1,1,2,4096]{3,2,1,0:T(2,128)(2,1)S(1)} all-reduce(bf16[1,1,2,4096]{3,2,1,0:T(2,128)(2,1)S(1)} %broadcast_select_fusion.2), channel_id=1, replica_groups=mesh['chan'=32,'day'=8] {'chan'}, use_global_device_ids=true, to_apply=%region_1.1 | all-reduce | flops 8192 | bytes 32768 | tf_op jit(solution)/shard_map/while/body/eval_jaxpr/psum | solution.py:13
  127.2 104.5 %psum.39 = bf16[1,1,2,4096]{3,2,1,0:T(2,128)(2,1)S(1)} all-reduce(bf16[1,1,2,4096]{3,2,1,0:T(2,128)(2,1)S(1)} %broadcast_select_fusion.2), channel_id=1, replica_groups=mesh['chan'=32,'day'=8] {'chan'}, use_global_device_ids=true, to_apply=%region_1.1 | all-reduce | flops 8192 | bytes 32768 | tf_op jit(solution)/shard_map/while/body/eval_jaxpr/psum | solution.py:13
  236.9 104.5 %psum.39 = bf16[1,1,2,4096]{3,2,1,0:T(2,128)(2,1)S(1)} all-reduce(bf16[1,1,2,4096]{3,2,1,0:T(2,128)(2,1)S(1)} %broadcast_select_fusion.2), channel_id=1, replica_groups=mesh['chan'=32,'day'=8] {'chan'}, use_global_device_ids=true, to_apply=%region_1.1 | all-reduce | flops 8192 | bytes 32768 | tf_op jit(solution)/shard_map/while/body/eval_jaxpr/psum | solution.py:13
  346.7 104.5 %psum.39 = bf16[1,1,2,4096]{3,2,1,0:T(2,128)(2,1)S(1)} all-reduce(bf16[1,1,2,4096]{3,2,1,0:T(2,128)(2,1)S(1)} %broadcast_select_fusion.2), channel_id=1, replica_groups=mesh['chan'=32,'day'=8] {'chan'}, use_global_device_ids=true, to_apply=%region_1.1 | all-reduce | flops 8192 | bytes 32768 | tf_op jit(solution)/shard_map/while/body/eval_jaxpr/psum | solution.py:13
  451.1 1.2 dynamic_slice.29
  456.4 104.5 %psum.39 = bf16[1,1,2,4096]{3,2,1,0:T(2,128)(2,1)S(1)} all-reduce(bf16[1,1,2,4096]{3,2,1,0:T(2,128)(2,1)S(1)} %broadcast_select_fusion.2), channel_id=1, replica_groups=mesh['chan'=32,'day'=8] {'chan'}, use_global_device_ids=true, to_apply=%region_1.1 | all-reduce | flops 8192 | bytes 32768 | tf_op jit(solution)/shard_map/while/body/eval_jaxpr/psum | solution.py:13
  566.1 104.5 %psum.39 = bf16[1,1,2,4096]{3,2,1,0:T(2,128)(2,1)S(1)} all-reduce(bf16[1,1,2,4096]{3,2,1,0:T(2,128)(2,1)S(1)} %broadcast_select_fusion.2), channel_id=1, replica_groups=mesh['chan'=32,'day'=8] {'chan'}, use_global_device_ids=true, to_apply=%region_1.1 | all-reduce | flops 8192 | bytes 32768 | tf_op jit(solution)/shard_map/while/body/eval_jaxpr/psum | solution.py:13
  675.9 104.5 %psum.39 = bf16[1,1,2,4096]{3,2,1,0:T(2,128)(2,1)S(1)} all-reduce(bf16[1,1,2,4096]{3,2,1,0:T(2,128)(2,1)S(1)} %broadcast_select_fusion.2), channel_id=1, replica_groups=mesh['chan'=32,'day'=8] {'chan'}, use_global_device_ids=true, to_apply=%region_1.1 | all-reduce | flops 8192 | bytes 32768 | tf_op jit(solution)/shard_map/while/body/eval_jaxpr/psum | solution.py:13
  785.6 104.5 %psum.39 = bf16[1,1,2,4096]{3,2,1,0:T(2,128)(2,1)S(1)} all-reduce(bf16[1,1,2,4096]{3,2,1,0:T(2,128)(2,1)S(1)} %broadcast_select_fusion.2), channel_id=1, replica_groups=mesh['chan'=32,'day'=8] {'chan'}, use_global_device_ids=true, to_apply=%region_1.1 | all-reduce | flops 8192 | bytes 32768 | tf_op jit(solution)/shard_map/while/body/eval_jaxpr/psum | solution.py:13
  895.3 104.5 %psum.39 = bf16[1,1,2,4096]{3,2,1,0:T(2,128)(2,1)S(1)} all-reduce(bf16[1,1,2,4096]{3,2,1,0:T(2,128)(2,1)S(1)} %broadcast_select_fusion.2), channel_id=1, replica_groups=mesh['chan'=32,'day'=8] {'chan'}, use_global_device_ids=true, to_apply=%region_1.1 | all-reduce | flops 8192 | bytes 32768 | tf_op jit(solution)/shard_map/while/body/eval_jaxpr/psum | solution.py:13
  1005.1 104.5 %psum.39 = bf16[1,1,2,4096]{3,2,1,0:T(2,128)(2,1)S(1)} all-reduce(bf16[1,1,2,4096]{3,2,1,0:T(2,128)(2,1)S(1)} %broadcast_select_fusion.2), channel_id=1, replica_groups=mesh['chan'=32,'day'=8] {'chan'}, use_global_device_ids=true, to_apply=%region_1.1 | all-reduce | flops 8192 | bytes 32768 | tf_op jit(solution)/shard_map/while/body/eval_jaxpr/psum | solution.py:13
  1114.8 104.5 %psum.39 = bf16[1,1,2,4096]{3,2,1,0:T(2,128)(2,1)S(1)} all-reduce(bf16[1,1,2,4096]{3,2,1,0:T(2,128)(2,1)S(1)} %broadcast_select_fusion.2), channel_id=1, replica_groups=mesh['chan'=32,'day'=8] {'chan'}, use_global_device_ids=true, to_apply=%region_1.1 | all-reduce | flops 8192 | bytes 32768 | tf_op jit(solution)/shard_map/while/body/eval_jaxpr/psum | solution.py:13
  1224.5 104.5 %psum.39 = bf16[1,1,2,4096]{3,2,1,0:T(2,128)(2,1)S(1)} all-reduce(bf16[1,1,2,4096]{3,2,1,0:T(2,128)(2,1)S(1)} %broadcast_select_fusion.2), channel_id=1, replica_groups=mesh['chan'=32,'day'=8] {'chan'}, use_global_device_ids=true, to_apply=%region_1.1 | all-reduce | flops 8192 | bytes 32768 | tf_op jit(solution)/shard_map/while/body/eval_jaxpr/psum | solution.py:13
  1334.3 104.5 %psum.39 = bf16[1,1,2,4096]{3,2,1,0:T(2,128)(2,1)S(1)} all-reduce(bf16[1,1,2,4096]{3,2,1,0:T(2,128)(2,1)S(1)} %broadcast_select_fusion.2), channel_id=1, replica_groups=mesh['chan'=32,'day'=8] {'chan'}, use_global_device_ids=true, to_apply=%region_1.1 | all-reduce | flops 8192 | bytes 32768 | tf_op jit(solution)/shard_map/while/body/eval_jaxpr/psum | solution.py:13
  1444.0 104.5 %psum.39 = bf16[1,1,2,4096]{3,2,1,0:T(2,128)(2,1)S(1)} all-reduce(bf16[1,1,2,4096]{3,2,1,0:T(2,128)(2,1)S(1)} %broadcast_select_fusion.2), channel_id=1, replica_groups=mesh['chan'=32,'day'=8] {'chan'}, use_global_device_ids=true, to_apply=%region_1.1 | all-reduce | flops 8192 | bytes 32768 | tf_op jit(solution)/shard_map/while/body/eval_jaxpr/psum | solution.py:13
  1553.7 104.5 %psum.39 = bf16[1,1,2,4096]{3,2,1,0:T(2,128)(2,1)S(1)} all-reduce(bf16[1,1,2,4096]{3,2,1,0:T(2,128)(2,1)S(1)} %broadcast_select_fusion.2), channel_id=1, replica_groups=mesh['chan'=32,'day'=8] {'chan'}, use_global_device_ids=true, to_apply=%region_1.1 | all-reduce | flops 8192 | bytes 32768 | tf_op jit(solution)/shard_map/while/body/eval_jaxpr/psum | solution.py:13
  1663.5 104.5 %psum.39 = bf16[1,1,2,4096]{3,2,1,0:T(2,128)(2,1)S(1)} all-reduce(bf16[1,1,2,4096]{3,2,1,0:T(2,128)(2,1)S(1)} %broadcast_select_fusion.2), channel_id=1, replica_groups=mesh['chan'=32,'day'=8] {'chan'}, use_global_device_ids=true, to_apply=%region_1.1 | all-reduce | flops 8192 | bytes 32768 | tf_op jit(solution)/shard_map/while/body/eval_jaxpr/psum | solution.py:13
  1768.7 17.1 multiply_convert_fusion.1
  1787.6 1.9 fusion.3
  1789.7 85.9 %all-reduce.4.cloned.1.call-done = f32[16,16,256]{2,1,0:T(8,128)} async-done(((f32[16,16,256]{2,1,0:T(8,128)}), f32[16,16,256]{2,1,0:T(8,128)}) %all-reduce.4.cloned.1.call-update) | async-done | bytes 262160 | tf_op jit(solution)/shard_map/psum | solution.py:65
  1875.5 2.1 multiply_reduce_fusion
  1877.8 58.7 %all-reduce.1 = (f32[1,8]{1,0:T(1,128)S(1)}, f32[1,8]{1,0:T(1,128)S(1)}) all-reduce(f32[1,8]{1,0:T(1,128)S(1)} %bitcast.31, f32[1,8]{1,0:T(1,128)S(1)} %bitcast.30), channel_id=1, replica_groups=mesh['chan'=32,'day'=8] {'chan'}, use_global_device_ids=true, to_apply=%region_6.7 | all-reduce | flops 16 | bytes 128 | tf_op jit(solution)/shard_map/psum | solution.py:85
  (66 shorter events, 35.2 us)
Async XLA Ops:
  7.2 1868.4 %all-reduce.4.cloned.1.call-start = ((), (), s32[]{:S(2)}) async-start(), calls=%async_computation | async-start | bytes 524288 | tf_op jit(solution)/shard_map/psum | solution.py:65
  1787.6 2.0 copy-start
  1787.6 90.0 %copy-start.1 = (s32[16]{0:T(128)S(1)}, s32[16]{0:T(128)}, u32[]{:S(2)}) copy-start(s32[16]{0:T(128)} %param.8) | copy-start | bytes 196
Sparse Core Ops, SparseCore 0:
  1789.7 85.8 all-reduce.3
where the time goes:
time: 1950 us; the launch traced here: 1940 us
  blocking collectives  1730 us (89%)
  waiting for transfers between devices  85.9 us (4%)
  loops' own time  52.4 us (3%)
  other arithmetic  34.2 us (2%)
  local copies, waits for them, and re-layouts  22.6 us (1%)
    psum x16, blocking collectives, from_root(): return lax.psum(kept, axis)  1670 us
    psum x1, waiting for transfers between devices, per_device(): total = lax.psum(local_sum, 'day')  85.9 us
    psum x1, blocking collectives, per_device(): lax.psum((jnp.stack(numers, 0), jnp.stack(denoms, 0)), 'chan')  58.7 us
    another operation x1, loops' own time, per_device(): lax.fori_loop(0, nsrc, fetch, jnp.zeros((day_dev, nsrc, 2, bins), jnp.bfl...  52.4 us
  transfers between devices with their start and end apart: 1, of which 1 were waited for; matrix products, arithmetic and copies ran while one was open for 0% of the time, Pallas kernels for 0%

commit v1 on v0

--- a/solution.py
+++ b/solution.py
@@ -10,7 +10,7 @@
 
 def from_root(value, axis, source):
     kept = jnp.where(lax.axis_index(axis) == source, value, 0).astype(value.dtype)
-    return lax.psum(kept, axis)
+    return jnp.sum(lax.all_gather(kept, axis), axis=0)
 
 
 def lag_table(bins, lags):

time: 1950 us -> 807 us (0.41)
  blocking collectives: 1730 us -> 591 us
    psum x16 -> x0, blocking collectives: 1670 us -> none  [from_root(): return lax.psum(kept, axis)]
    all_gather x0 -> x16, blocking collectives: none -> 532 us  [from_root(): return jnp.sum(lax.all_gather(kept, axis), axis=0)]
where the time goes in v1:
time: 807 us; the launch traced here: 804 us
  blocking collectives  591 us (73%)
  waiting for transfers between devices  80.6 us (10%)
  loops' own time  52.5 us (7%)
  other arithmetic  41.2 us (5%)
  local copies, waits for them, and re-layouts  22.6 us (3%)
  between operations  14.2 us (2%)
    all_gather x16, blocking collectives, from_root(): return jnp.sum(lax.all_gather(kept, axis), axis=0)  532 us
    psum x1, waiting for transfers between devices, per_device(): total = lax.psum(local_sum, 'day')  80.6 us
    psum x1, blocking collectives, per_device(): lax.psum((jnp.stack(numers, 0), jnp.stack(denoms, 0)), 'chan')  58.7 us
    another operation x1, loops' own time, per_device(): lax.fori_loop(0, nsrc, fetch, jnp.zeros((day_dev, nsrc, 2, bins), jnp.bfl...  52.5 us
    dynamic_slice x16, local copies, waits for them, and re-layouts, fetch(): chosen_chan = source_index[source]  19.9 us
    another operation x2, other arithmetic  18.2 us
  transfers between devices with their start and end apart: 1, of which 1 were waited for; matrix products, arithmetic and copies ran while one was open for 0% of the time, Pallas kernels for 0%

profile of v1, /device:TPU:1, one launch (start us, length us, event | category | flops | bytes accessed | tf_op | source)
XLA Modules:
  0.0 803.9 jit_solution(11513031456762426176)
XLA Ops:
  9.0 623.7 %while.20 = (s32[]{:T(128)}, bf16[1,16,2,4096]{3,2,1,0:T(2,128)(2,1)S(1)}, s32[16]{0:T(128)}, bf16[1,16,2,4096]{3,2,1,0:T(2,128)(2,1)}, s32[]{:T(128)}, /*index=...) while((s32[]{:T(128)}, ...), condition=%wide.region_2.3_spmd, body=%wide.region_0.2_spmd.sunk | while | flops 262170 | bytes 1147277 | solution.py:40
  9.0 1.2 dynamic_slice.31
  14.2 39.9 %all-gather.2 = bf16[32,1,2,4096]{3,2,1,0:T(2,128)(2,1)S(1)} all-gather(bf16[1,1,2,4096]{3,2,1,0:T(2,128)(2,1)S(1)} %broadcast_select_fusion.2), channel_id=2, replica_groups=mesh['chan'=32,'day'=8] {'chan'}, dimensions={0}, use_global_device_ids=true | all-gather | bytes 540672 | tf_op jit(solution)/shard_map/while/body/eval_jaxpr/all_gather | solution.py:13
  59.8 32.1 %all-gather.2 = bf16[32,1,2,4096]{3,2,1,0:T(2,128)(2,1)S(1)} all-gather(bf16[1,1,2,4096]{3,2,1,0:T(2,128)(2,1)S(1)} %broadcast_select_fusion.2), channel_id=2, replica_groups=mesh['chan'=32,'day'=8] {'chan'}, dimensions={0}, use_global_device_ids=true | all-gather | bytes 540672 | tf_op jit(solution)/shard_map/while/body/eval_jaxpr/all_gather | solution.py:13
  97.7 33.6 %all-gather.2 = bf16[32,1,2,4096]{3,2,1,0:T(2,128)(2,1)S(1)} all-gather(bf16[1,1,2,4096]{3,2,1,0:T(2,128)(2,1)S(1)} %broadcast_select_fusion.2), channel_id=2, replica_groups=mesh['chan'=32,'day'=8] {'chan'}, dimensions={0}, use_global_device_ids=true | all-gather | bytes 540672 | tf_op jit(solution)/shard_map/while/body/eval_jaxpr/all_gather | solution.py:13
  131.8 1.2 dynamic_slice.31
  137.0 32.1 %all-gather.2 = bf16[32,1,2,4096]{3,2,1,0:T(2,128)(2,1)S(1)} all-gather(bf16[1,1,2,4096]{3,2,1,0:T(2,128)(2,1)S(1)} %broadcast_select_fusion.2), channel_id=2, replica_groups=mesh['chan'=32,'day'=8] {'chan'}, dimensions={0}, use_global_device_ids=true | all-gather | bytes 540672 | tf_op jit(solution)/shard_map/while/body/eval_jaxpr/all_gather | solution.py:13
  174.8 33.6 %all-gather.2 = bf16[32,1,2,4096]{3,2,1,0:T(2,128)(2,1)S(1)} all-gather(bf16[1,1,2,4096]{3,2,1,0:T(2,128)(2,1)S(1)} %broadcast_select_fusion.2), channel_id=2, replica_groups=mesh['chan'=32,'day'=8] {'chan'}, dimensions={0}, use_global_device_ids=true | all-gather | bytes 540672 | tf_op jit(solution)/shard_map/while/body/eval_jaxpr/all_gather | solution.py:13
  214.2 32.1 %all-gather.2 = bf16[32,1,2,4096]{3,2,1,0:T(2,128)(2,1)S(1)} all-gather(bf16[1,1,2,4096]{3,2,1,0:T(2,128)(2,1)S(1)} %broadcast_select_fusion.2), channel_id=2, replica_groups=mesh['chan'=32,'day'=8] {'chan'}, dimensions={0}, use_global_device_ids=true | all-gather | bytes 540672 | tf_op jit(solution)/shard_map/while/body/eval_jaxpr/all_gather | solution.py:13
  252.0 33.6 %all-gather.2 = bf16[32,1,2,4096]{3,2,1,0:T(2,128)(2,1)S(1)} all-gather(bf16[1,1,2,4096]{3,2,1,0:T(2,128)(2,1)S(1)} %broadcast_select_fusion.2), channel_id=2, replica_groups=mesh['chan'=32,'day'=8] {'chan'}, dimensions={0}, use_global_device_ids=true | all-gather | bytes 540672 | tf_op jit(solution)/shard_map/while/body/eval_jaxpr/all_gather | solution.py:13
  291.4 32.1 %all-gather.2 = bf16[32,1,2,4096]{3,2,1,0:T(2,128)(2,1)S(1)} all-gather(bf16[1,1,2,4096]{3,2,1,0:T(2,128)(2,1)S(1)} %broadcast_select_fusion.2), channel_id=2, replica_groups=mesh['chan'=32,'day'=8] {'chan'}, dimensions={0}, use_global_device_ids=true | all-gather | bytes 540672 | tf_op jit(solution)/shard_map/while/body/eval_jaxpr/all_gather | solution.py:13
  329.2 33.6 %all-gather.2 = bf16[32,1,2,4096]{3,2,1,0:T(2,128)(2,1)S(1)} all-gather(bf16[1,1,2,4096]{3,2,1,0:T(2,128)(2,1)S(1)} %broadcast_select_fusion.2), channel_id=2, replica_groups=mesh['chan'=32,'day'=8] {'chan'}, dimensions={0}, use_global_device_ids=true | all-gather | bytes 540672 | tf_op jit(solution)/shard_map/while/body/eval_jaxpr/all_gather | solution.py:13
  368.5 32.1 %all-gather.2 = bf16[32,1,2,4096]{3,2,1,0:T(2,128)(2,1)S(1)} all-gather(bf16[1,1,2,4096]{3,2,1,0:T(2,128)(2,1)S(1)} %broadcast_select_fusion.2), channel_id=2, replica_groups=mesh['chan'=32,'day'=8] {'chan'}, dimensions={0}, use_global_device_ids=true | all-gather | bytes 540672 | tf_op jit(solution)/shard_map/while/body/eval_jaxpr/all_gather | solution.py:13
  406.4 33.6 %all-gather.2 = bf16[32,1,2,4096]{3,2,1,0:T(2,128)(2,1)S(1)} all-gather(bf16[1,1,2,4096]{3,2,1,0:T(2,128)(2,1)S(1)} %broadcast_select_fusion.2), channel_id=2, replica_groups=mesh['chan'=32,'day'=8] {'chan'}, dimensions={0}, use_global_device_ids=true | all-gather | bytes 540672 | tf_op jit(solution)/shard_map/while/body/eval_jaxpr/all_gather | solution.py:13
  445.7 32.1 %all-gather.2 = bf16[32,1,2,4096]{3,2,1,0:T(2,128)(2,1)S(1)} all-gather(bf16[1,1,2,4096]{3,2,1,0:T(2,128)(2,1)S(1)} %broadcast_select_fusion.2), channel_id=2, replica_groups=mesh['chan'=32,'day'=8] {'chan'}, dimensions={0}, use_global_device_ids=true | all-gather | bytes 540672 | tf_op jit(solution)/shard_map/while/body/eval_jaxpr/all_gather | solution.py:13
  483.6 33.6 %all-gather.2 = bf16[32,1,2,4096]{3,2,1,0:T(2,128)(2,1)S(1)} all-gather(bf16[1,1,2,4096]{3,2,1,0:T(2,128)(2,1)S(1)} %broadcast_select_fusion.2), channel_id=2, replica_groups=mesh['chan'=32,'day'=8] {'chan'}, dimensions={0}, use_global_device_ids=true | all-gather | bytes 540672 | tf_op jit(solution)/shard_map/while/body/eval_jaxpr/all_gather | solution.py:13
  522.9 32.1 %all-gather.2 = bf16[32,1,2,4096]{3,2,1,0:T(2,128)(2,1)S(1)} all-gather(bf16[1,1,2,4096]{3,2,1,0:T(2,128)(2,1)S(1)} %broadcast_select_fusion.2), channel_id=2, replica_groups=mesh['chan'=32,'day'=8] {'chan'}, dimensions={0}, use_global_device_ids=true | all-gather | bytes 540672 | tf_op jit(solution)/shard_map/while/body/eval_jaxpr/all_gather | solution.py:13
  560.7 33.6 %all-gather.2 = bf16[32,1,2,4096]{3,2,1,0:T(2,128)(2,1)S(1)} all-gather(bf16[1,1,2,4096]{3,2,1,0:T(2,128)(2,1)S(1)} %broadcast_select_fusion.2), channel_id=2, replica_groups=mesh['chan'=32,'day'=8] {'chan'}, dimensions={0}, use_global_device_ids=true | all-gather | bytes 540672 | tf_op jit(solution)/shard_map/while/body/eval_jaxpr/all_gather | solution.py:13
  600.1 32.1 %all-gather.2 = bf16[32,1,2,4096]{3,2,1,0:T(2,128)(2,1)S(1)} all-gather(bf16[1,1,2,4096]{3,2,1,0:T(2,128)(2,1)S(1)} %broadcast_select_fusion.2), channel_id=2, replica_groups=mesh['chan'=32,'day'=8] {'chan'}, dimensions={0}, use_global_device_ids=true | all-gather | bytes 540672 | tf_op jit(solution)/shard_map/while/body/eval_jaxpr/all_gather | solution.py:13
  633.5 17.1 %multiply_convert_fusion.1 = (bf16[4096,256]{1,0:T(8,128)(2,1)S(1)}, bf16[4096,256]{1,0:T(8,128)(2,1)S(1)}) fusion(s32[256]{0:T(256)S(1)} %iota_add_fusion), kind=kLoop, calls=%fused_computation.16 | loop fusion | flops 19922944 | bytes 4195328 | tf_op jit(solution)/shard_map/convert.7
  652.4 1.9 fusion.3
  654.4 80.6 %all-reduce.4.cloned.1.call-done = f32[16,16,256]{2,1,0:T(8,128)} async-done(((f32[16,16,256]{2,1,0:T(8,128)}), f32[16,16,256]{2,1,0:T(8,128)}) %all-reduce.4.cloned.1.call-update) | async-done | bytes 262160 | tf_op jit(solution)/shard_map/psum | solution.py:65
  735.0 2.1 multiply_reduce_fusion
  737.3 58.7 %all-reduce.1 = (f32[1,8]{1,0:T(1,128)S(1)}, f32[1,8]{1,0:T(1,128)S(1)}) all-reduce(f32[1,8]{1,0:T(1,128)S(1)} %bitcast.35, f32[1,8]{1,0:T(1,128)S(1)} %bitcast.34), channel_id=1, replica_groups=mesh['chan'=32,'day'=8] {'chan'}, use_global_device_ids=true, to_apply=%region_6.7 | all-reduce | flops 16 | bytes 128 | tf_op jit(solution)/shard_map/psum | solution.py:85
  (82 shorter events, 42.1 us)
Async XLA Ops:
  7.2 727.9 %all-reduce.4.cloned.1.call-start = ((), (), s32[]{:S(2)}) async-start(), calls=%async_computation | async-start | bytes 524288 | tf_op jit(solution)/shard_map/psum | solution.py:65
  652.3 2.0 copy-start
  652.3 84.8 %copy-start.1 = (s32[16]{0:T(128)S(1)}, s32[16]{0:T(128)}, u32[]{:S(2)}) copy-start(s32[16]{0:T(128)} %param.8) | copy-start | bytes 196
Sparse Core Ops, SparseCore 0:
  654.4 80.5 all-reduce.3
